TPU v7x, 512 devices: a whole 4x8x8 slice. The times are simulated.
512 devices in a mesh: ctx: 64 (over z, y), tp: 8 (over x, core).
Axes of the slice: x: 4, y: 8, z: 8, core: 2. Of those that a mesh axis runs over, the one named last changes fastest.
Arguments:
- span_q: bfloat16 [8192, 8192], P('ctx', 'tp'), may hold values from -21 to 21
- span_kv: bfloat16 [2, 8192, 1024], P(None, 'ctx', 'tp'), may hold values from -20 to 20
- cache_kv: bfloat16 [2, 65536, 1024], P(None, 'ctx', 'tp'), may hold values from -20 to 20
- anchor_kv: bfloat16 [2, 2048, 1024], P(None, 'ctx', 'tp'), may hold values from -20 to 20
- block_len: int32 [64], P('ctx'), may hold values from 1 to 1024, 40960 in all
- queries: bfloat16 [128, 8192], P('ctx', 'tp'), may hold values from -21 to 21
- out_weight: bfloat16 [8192, 8192], P('tp', 'ctx'), may hold values from -0.0625 to 0.0625
Outputs:
- span_out: bfloat16 [8192, 8192], P('ctx', 'tp')
- answer: bfloat16 [128, 8192], P('tp', 'ctx')
Inputs may be any that keep to these rules, and one draw needn't show every extreme that they name: The new tokens of block c follow its block_len[c] valid cache rows.
All inputs are finite; a program needn't handle non-finite values.
Results may differ from a plain program's by a relative error of at most 0.0049.
Values may be sent and summed in bfloat16 or wider, within the bound.
A program may use at most 64 MiB of HBM per device.

v0:
```python
import math
import jax
import jax.numpy as jnp
from jax import lax
from jax.sharding import PartitionSpec as P

HD = 128
masked_score = -1e30


def all_heads(query_rows, key_rows, value_rows, visible):
    row_count = query_rows.shape[0]
    head_count = query_rows.shape[1] // HD
    score_scale = 1.0 / math.sqrt(HD)

    def per_head(head_index, running):
        maxima, totals, outputs = running
        q_head = lax.dynamic_slice_in_dim(query_rows, head_index * HD, HD, 1)
        scores = (
            jnp.einsum("qd,nd->qn", q_head, key_rows, preferred_element_type=jnp.float32)
            * score_scale
        )
        scores = jnp.where(visible, scores, masked_score)
        peak_score = jnp.max(scores, axis=1, keepdims=True)
        weights = jnp.exp(scores - peak_score)
        weight_sum = jnp.sum(weights, axis=1, keepdims=True)
        product = jnp.einsum(
            "qn,nd->qd",
            weights.astype(jnp.bfloat16),
            value_rows,
            preferred_element_type=jnp.float32,
        )
        maxima = lax.dynamic_update_slice_in_dim(maxima, peak_score, head_index, 1)
        totals = lax.dynamic_update_slice_in_dim(totals, weight_sum, head_index, 1)
        outputs = lax.dynamic_update_slice_in_dim(outputs, product, head_index * HD, 1)
        return (maxima, totals, outputs)

    initial = (
        jnp.zeros((row_count, head_count), jnp.float32),
        jnp.zeros((row_count, head_count), jnp.float32),
        jnp.zeros((row_count, head_count * HD), jnp.float32),
    )
    return lax.fori_loop(0, head_count, per_head, initial)


def local(span_q, span_kv, cache_kv, anchor_kv, block_len, queries, out_weight):
    cache_count = cache_kv.shape[1]
    span_count = span_kv.shape[1]
    length = block_len[0]
    local_kv = jnp.concatenate([cache_kv, span_kv], axis=1)
    anchor_all = lax.all_gather(anchor_kv, "ctx", axis=1, tiled=True)
    query_all = lax.all_gather(queries, "ctx", axis=0, tiled=True)
    anchor_count = anchor_all.shape[1]
    first_kv = jnp.concatenate([anchor_all, local_kv], axis=1)
    key_total = first_kv.shape[1]
    column = lax.broadcasted_iota(jnp.int32, (span_count, key_total), 1)
    query_pos = lax.broadcasted_iota(jnp.int32, (span_count, key_total), 0)
    in_cache = (column >= anchor_count) & (column < anchor_count + cache_count)
    in_span = column >= anchor_count + cache_count
    visible = jnp.where(
        in_cache,
        column - anchor_count < length,
        jnp.where(in_span, column - anchor_count - cache_count <= query_pos, True),
    )
    first_max, first_sum, first_values = all_heads(span_q, first_kv[0], first_kv[1], visible)
    span_out = (first_values / jnp.repeat(first_sum, HD, axis=1)).astype(jnp.bfloat16)
    own_count = anchor_kv.shape[1]
    second_kv = jnp.concatenate([anchor_kv, local_kv], axis=1)
    column_two = lax.broadcasted_iota(jnp.int32, (1, second_kv.shape[1]), 1)
    cache_two = (column_two >= own_count) & (column_two < own_count + cache_count)
    visible_two = jnp.where(cache_two, column_two - own_count < length, True)
    part_max, part_sum, part_values = all_heads(query_all, second_kv[0], second_kv[1], visible_two)
    global_max = lax.pmax(part_max, "ctx")
    rescale = jnp.exp(part_max - global_max)
    full_sum, full_values = lax.psum(
        (part_sum * rescale, part_values * jnp.repeat(rescale, HD, axis=1)), "ctx"
    )
    attended = (full_values / jnp.repeat(full_sum, HD, axis=1)).astype(jnp.bfloat16)
    partial_value = jnp.dot(attended, out_weight, preferred_element_type=jnp.float32)
    answer = lax.psum_scatter(partial_value, "tp", scatter_dimension=0, tiled=True).astype(
        jnp.bfloat16
    )
    return (span_out, answer)


def solution(mesh):
    placed = (
        P("ctx", "tp"),
        P(None, "ctx", "tp"),
        P(None, "ctx", "tp"),
        P(None, "ctx", "tp"),
        P("ctx"),
        P("ctx", "tp"),
        P("tp", "ctx"),
    )
    return jax.shard_map(
        local,
        mesh=mesh,
        in_specs=placed,
        out_specs=(P("ctx", "tp"), P("tp", "ctx")),
        check_vma=False,
    )
```

profile of v0, /device:TPU:16, one launch (start us, length us, event | category | flops | bytes accessed | tf_op | source)
XLA Modules:
  0.0 452.8 jit_solution(17501054155772972104)
XLA Ops:
  8.0 56.4 %all-gather = bf16[64,2,1024]{2,1,0:T(2,128)(2,1)S(1)} all-gather(bf16[1,2,1024]{2,1,0:T(2,128)(2,1)} %bitcast.53), channel_id=1, replica_groups=mesh['ctx'=64,'tp'=8] {'ctx'}, dimensions={0}, use_global_device_ids=true | all-gather | bytes 266240 | tf_op jit(solution)/shard_map/all_gather | solution.py:52
  65.2 0.7 constant_dynamic-update-slice_fusion.5
  66.5 27.6 %all-gather.3.cloned.1.call-done = bf16[2,2048,128]{2,1,0:T(8,128)(2,1)} async-done(((bf16[2,32,128]{2,1,0:T(8,128)(2,1)}), bf16[2,2048,128]{2,1,0:T(8,128)(2,1)}) %all-gather.3.cloned.1.call-update) | async-done | bytes 1048592 | tf_op jit(solution)/shard_map/all_gather | solution.py:51
  94.1 1.3 constant_dynamic-update-slice_fusion.2
  95.7 0.8 copy-done.1
  96.5 1.1 slice_bitcast_fusion.2
  97.6 13.0 %while.35 = (s32[]{:T(128)}, f32[128,8]{0,1:T(8,128)S(1)}, f32[128,8]{0,1:T(8,128)S(1)}, f32[128,1024]{1,0:T(8,128)S(1)}, bf16[128,1024]{1,0:T(8,128)(2,1)S(1)},...) while((s32[]{:T(128)}, f32[128,8]{0,1:T(8,128)S(1)}, ...), condition=%wide.region_7.8_spmd.clone, body=%wide.region_4.7_spmd.clone.sunk | while | flops 78662336 | bytes 2530647 | solution.py:43
  97.7 0.7 select_reduce_fusion.2
  110.6 137.7 %pmax.7 = f32[128,8]{0,1:T(8,128)S(1)} all-reduce(f32[128,8]{0,1:T(8,128)S(1)} %get-tuple-element.271), channel_id=1, replica_groups=mesh['ctx'=64,'tp'=8] {'ctx'}, use_global_device_ids=true, to_apply=%region_8.9 | all-reduce | flops 1024 | bytes 8192 | tf_op jit(solution)/shard_map/pmax | solution.py:73
  248.6 0.9 bitcast_multiply_fusion
  249.8 19.4 %while.34 = (s32[]{:T(128)}, f32[128,8]{0,1:T(8,128)S(1)}, f32[128,1024]{1,0:T(8,128)S(1)}, bf16[128,1024]{1,0:T(8,128)(2,1)}, bf16[3200,128]{1,0:T(8,128)(2,1)S...) while((s32[]{:T(128)}, f32[128,8]{0,1:T(8,128)S(1)}, ...), condition=%wide.region_3.4_spmd.clone, body=%wide.region_0.3_spmd.clone.sunk | while | flops 213810944 | bytes 6681151 | solution.py:43
  249.9 1.5 fusion.46
  252.3 1.5 fusion.46
  254.7 1.5 fusion.46
  257.1 1.5 fusion.46
  259.5 1.5 fusion.46
  262.0 1.5 fusion.46
  264.4 1.5 fusion.46
  266.8 1.5 fusion.46
  269.2 138.1 %psum.15 = f32[128,8]{0,1:T(8,128)S(1)} all-reduce(f32[128,8]{0,1:T(8,128)S(1)} %get-tuple-element.354), channel_id=1, replica_groups=mesh['ctx'=64,'tp'=8] {'ctx'}, use_global_device_ids=true, to_apply=%region_10.11 | all-reduce | flops 1024 | bytes 8192 | tf_op jit(solution)/shard_map/psum | solution.py:75
  407.7 1.9 fusion.22
  409.8 0.8 fusion.21
  410.6 34.3 %reduce-scatter.2.cloned.1.call-done = f32[16,128]{1,0:T(8,128)} async-done(((f32[128,128]{1,0:T(8,128)}), f32[16,128]{1,0:T(8,128)}) %reduce-scatter.2.cloned.1.call-update) | async-done | bytes 8208 | tf_op jit(solution)/shard_map/reduce_scatter | solution.py:80
  444.9 1.3 convert_element_type.25
  (104 shorter events, 21.9 us)
Async XLA Ops:
  7.2 400.5 %copy-start = (bf16[1024,128]{1,0:T(8,128)(2,1)S(1)}, bf16[1024,128]{1,0:T(8,128)(2,1)}, u32[]{:S(2)}) copy-start(bf16[1024,128]{1,0:T(8,128)(2,1)} %param.17) | copy-start | bytes 786436
  7.2 88.2 %copy-start.2 = (bf16[2,1024,128]{2,1,0:T(8,128)(2,1)S(1)}, bf16[2,1024,128]{2,1,0:T(8,128)(2,1)}, u32[]{:S(2)}) copy-start(bf16[2,1024,128]{2,1,0:T(8,128)(2,1)} %param.13) | copy-start | bytes 1572868
  7.2 86.9 %all-gather.3.cloned.1.call-start = ((), (), s32[]{:S(2)}) async-start(), calls=%async_computation.1 | async-start | bytes 1064960 | tf_op jit(solution)/shard_map/all_gather | solution.py:51
  7.9 399.6 %all-reduce.2.cloned.1.call-start = ((), (), s32[]{:S(2)}) async-start(), calls=%async_computation.2 | async-start | bytes 1048576 | tf_op jit(solution)/shard_map/psum | solution.py:75
  66.5 29.1 %copy-start.3 = (bf16[2,128,128]{2,1,0:T(8,128)(2,1)S(1)}, bf16[2,128,128]{2,1,0:T(8,128)(2,1)}, u32[]{:S(2)}) copy-start(bf16[2,128,128]{2,1,0:T(8,128)(2,1)} %param.12) | copy-start | bytes 196612
  95.7 0.8 copy-start.1
  249.6 195.3 %reduce-scatter.2.cloned.1.call-start = ((), (), s32[]{:S(2)}) async-start(), calls=%async_computation.3 | async-start | bytes 73728 | tf_op jit(solution)/shard_map/reduce_scatter | solution.py:80
Sparse Core Ops, SparseCore 0:
  11.0 83.0 all-gather.2
  249.7 155.1 all-reduce.1
  409.7 35.1 reduce-scatter.1
where the time goes:
time: 454 us; the launch traced here: 453 us
  blocking collectives  332 us (73%)
  waiting for transfers between devices  62.6 us (14%)
  matrix products  23.1 us (5%)
  between operations  14.6 us (3%)
  other arithmetic  13.6 us (3%)
  local copies, waits for them, and re-layouts  6.12 us (1%)
    psum x1, blocking collectives, local(): lax.psum((part_sum * rescale, part_values * jnp.repeat(rescale, HD, axis=...  138 us
    pmax x1, blocking collectives, local(): global_max = lax.pmax(part_max, 'ctx')  138 us
    all_gather x1, blocking collectives, local(): query_all = lax.all_gather(queries, 'ctx', axis=0, tiled=True)  56.4 us
    reduce_scatter x1, waiting for transfers between devices, local(): lax.psum_scatter(partial_value, 'tp', scatter_dimension=0, tiled=True)  34.3 us
    all_gather x1, waiting for transfers between devices, local(): anchor_all = lax.all_gather(anchor_kv, 'ctx', axis=1, tiled=True)  27.6 us
    dot_general x16, matrix products, per_head(): jnp.einsum('qd,nd->qn', q_head, key_rows, preferred_element_type=jnp.floa...  15.1 us
  transfers between devices with their start and end apart: 3, of which 2 were waited for; matrix products, arithmetic and copies ran while one was open for 5% of the time, Pallas kernels for 0%

commit v1 on v0

--- a/solution.py
+++ b/solution.py
@@ -48,7 +48,13 @@
     span_count = span_kv.shape[1]
     length = block_len[0]
     local_kv = jnp.concatenate([cache_kv, span_kv], axis=1)
-    anchor_all = lax.all_gather(anchor_kv, "ctx", axis=1, tiled=True)
+
+    def turn_domain(point, dev_axis, at_axis):
+        plain = jnp.stack([point for _ in range(lax.psum(1, dev_axis))])
+        finding = lax.all_to_all(plain, dev_axis, 0, 0)
+        return jnp.concatenate(finding, at_axis)
+
+    anchor_all = turn_domain(anchor_kv, "ctx", 1)
     query_all = lax.all_gather(queries, "ctx", axis=0, tiled=True)
     anchor_count = anchor_all.shape[1]
     first_kv = jnp.concatenate([anchor_all, local_kv], axis=1)

time: 454 us -> 477 us (1.051)
  the two profiles are of different devices: /device:TPU:16 before, /device:TPU:8 now
where the time goes in v1:
time: 477 us
  blocking collectives  347 us (73%)
  waiting for transfers between devices  45.4 us (10%)
  matrix products  31.2 us (7%)
  starting transfers between devices  16.8 us (4%)
  other arithmetic  15.4 us (3%)
  between operations  14.9 us (3%)
  local copies, waits for them, and re-layouts  5.87 us (1%)
    psum x1, blocking collectives, local(): lax.psum((part_sum * rescale, part_values * jnp.repeat(rescale, HD, axis=...  141 us
    pmax x1, blocking collectives, local(): global_max = lax.pmax(part_max, 'ctx')  138 us
    all_gather x1, blocking collectives, local(): query_all = lax.all_gather(queries, 'ctx', axis=0, tiled=True)  67.7 us
    reduce_scatter x1, waiting for transfers between devices, local(): lax.psum_scatter(partial_value, 'tp', scatter_dimension=0, tiled=True)  33.5 us
    dot_general x16, matrix products, per_head(): jnp.einsum('qd,nd->qn', q_head, key_rows, preferred_element_type=jnp.floa...  18.3 us
    all_to_all x1, starting transfers between devices, turn_domain(): finding = lax.all_to_all(plain, dev_axis, 0, 0)  16.7 us
    psum x1, waiting for transfers between devices, local(): lax.psum((part_sum * rescale, part_values * jnp.repeat(rescale, HD, axis=...  11.8 us
    dot_general x16, matrix products, per_head(): jnp.einsum('qn,nd->qd', weights.astype(jnp.bfloat16), value_rows, preferr...  11.1 us
  transfers between devices with their start and end apart: 3, of which 2 were waited for; matrix products, arithmetic and copies ran while one was open for 5% of the time, Pallas kernels for 0%

profile of v1, /device:TPU:8, one launch (start us, length us, event | category | flops | bytes accessed | tf_op | source)
XLA Modules:
  0.0 476.6 jit_solution(17999498950630288683)
XLA Ops:
  7.2 2.0 stack.2
  9.2 16.7 %all-to-all-start = ((bf16[64,2,32,128]{3,2,1,0:T(8,128)(2,1)}), bf16[64,2,32,128]{3,2,1,0:T(8,128)(2,1)S(1)}, u32[]{:S(2)}, u32[]{:S(2)}) async-start(bf16[64,2,32,128]{3,2,1,0:T(8,128)(2,1)} %stack.2), calls=%async_computation | async-start | bytes 2097152 | tf_op jit(solution)/shard_map/all_to_all | solution.py:54
  26.0 67.7 %all-gather = bf16[64,2,1024]{2,1,0:T(2,128)(2,1)S(1)} all-gather(bf16[1,2,1024]{2,1,0:T(2,128)(2,1)S(1)} %bitcast.57), channel_id=1, replica_groups=mesh['ctx'=64,'tp'=8] {'ctx'}, dimensions={0}, use_global_device_ids=true | all-gather | bytes 266240 | tf_op jit(solution)/shard_map/all_gather | solution.py:58
  94.9 17.8 %while.35 = (s32[]{:T(128)}, f32[128,8]{0,1:T(8,128)S(1)}, f32[128,8]{0,1:T(8,128)S(1)}, f32[128,1024]{1,0:T(8,128)}, bf16[128,1024]{1,0:T(8,128)(2,1)S(1)}, /*i...) while((s32[]{:T(128)}, f32[128,8]{0,1:T(8,128)S(1)}, ...), condition=%wide.region_7.8_spmd.clone, body=%wide.region_4.7_spmd.clone.sunk | while | flops 78662336 | bytes 2530655 | solution.py:43
  105.1 0.9 convolution_dynamic-update-slice_fusion.5
  107.3 0.9 convolution_dynamic-update-slice_fusion.5
  111.7 1.0 convolution_dynamic-update-slice_fusion.5
  112.7 137.9 %pmax.7 = f32[128,8]{0,1:T(8,128)S(1)} all-reduce(f32[128,8]{0,1:T(8,128)S(1)} %get-tuple-element.271), channel_id=1, replica_groups=mesh['ctx'=64,'tp'=8] {'ctx'}, use_global_device_ids=true, to_apply=%region_8.9 | all-reduce | flops 1024 | bytes 8192 | tf_op jit(solution)/shard_map/pmax | solution.py:79
  250.9 2.0 bitcast_multiply_fusion
  253.6 141.2 %psum.15 = f32[128,8]{0,1:T(8,128)S(1)} all-reduce(f32[128,8]{0,1:T(8,128)S(1)} %get-tuple-element.354), channel_id=1, replica_groups=mesh['ctx'=64,'tp'=8] {'ctx'}, use_global_device_ids=true, to_apply=%region_10.11 | all-reduce | flops 1024 | bytes 8192 | tf_op jit(solution)/shard_map/psum | solution.py:81
  395.5 11.8 %all-reduce.2.cloned.1.call-done = f32[128,1024]{1,0:T(8,128)} async-done(((f32[128,1024]{1,0:T(8,128)}), f32[128,1024]{1,0:T(8,128)}) %all-reduce.2.cloned.1.call-update) | async-done | bytes 524304 | tf_op jit(solution)/shard_map/psum | solution.py:81
  407.5 1.9 fusion.22
  410.0 33.5 %reduce-scatter.2.cloned.1.call-done = f32[16,128]{1,0:T(8,128)} async-done(((f32[128,128]{1,0:T(8,128)}), f32[16,128]{1,0:T(8,128)}) %reduce-scatter.2.cloned.1.call-update) | async-done | bytes 8208 | tf_op jit(solution)/shard_map/reduce_scatter | solution.py:86
  443.6 1.3 convert_element_type.25
  445.1 1.0 slice_bitcast_fusion
  446.2 22.5 %while.34 = (s32[]{:T(128)}, f32[128,8]{0,1:T(8,128)S(1)}, f32[128,1024]{1,0:T(8,128)S(1)}, bf16[128,1024]{1,0:T(8,128)(2,1)}, bf16[3200,128]{1,0:T(8,128)(2,1)}...) while((s32[]{:T(128)}, f32[128,8]{0,1:T(8,128)S(1)}, ...), condition=%wide.region_3.4_spmd.clone, body=%wide.region_0.3_spmd.clone.sunk | while | flops 213810944 | bytes 6677575 | solution.py:43
  446.2 1.9 fusion.46
  449.0 1.9 fusion.46
  451.8 1.9 fusion.46
  454.6 1.9 fusion.46
  457.4 1.9 fusion.46
  460.2 1.9 fusion.46
  463.0 1.9 fusion.46
  465.9 1.9 fusion.46
  (113 shorter events, 26.2 us)
Async XLA Ops:
  7.2 400.3 %copy-start = (bf16[1024,128]{1,0:T(8,128)(2,1)S(1)}, bf16[1024,128]{1,0:T(8,128)(2,1)}, u32[]{:S(2)}) copy-start(bf16[1024,128]{1,0:T(8,128)(2,1)} %param.17) | copy-start | bytes 786436
  7.2 18.8 %copy-start.3 = (bf16[2,32,128]{2,1,0:T(8,128)(2,1)S(1)}, bf16[2,32,128]{2,1,0:T(8,128)(2,1)}, u32[]{:S(2)}) copy-start(bf16[2,32,128]{2,1,0:T(8,128)(2,1)} %param.14) | copy-start | bytes 49156
  7.2 18.8 %copy-start.4 = (bf16[2,1024]{1,0:T(2,128)(2,1)S(1)}, bf16[2,1024]{1,0:T(2,128)(2,1)}, u32[]{:S(2)}) copy-start(bf16[2,1024]{1,0:T(2,128)(2,1)} %param.16) | copy-start | bytes 12292
  9.2 84.6 %copy-start.1 = (bf16[2,1024,128]{2,1,0:T(8,128)(2,1)S(1)}, bf16[2,1024,128]{2,1,0:T(8,128)(2,1)}, u32[]{:S(2)}) copy-start(bf16[2,1024,128]{2,1,0:T(8,128)(2,1)} %param.13) | copy-start | bytes 1572868
  9.2 84.7 %copy-start.2 = (bf16[2,128,128]{2,1,0:T(8,128)(2,1)S(1)}, bf16[2,128,128]{2,1,0:T(8,128)(2,1)}, u32[]{:S(2)}) copy-start(bf16[2,128,128]{2,1,0:T(8,128)(2,1)} %param.12) | copy-start | bytes 196612
  9.2 435.6 %all-to-all-start = ((bf16[64,2,32,128]{3,2,1,0:T(8,128)(2,1)}), bf16[64,2,32,128]{3,2,1,0:T(8,128)(2,1)S(1)}, u32[]{:S(2)}, u32[]{:S(2)}) async-start(bf16[64,2,32,128]{3,2,1,0:T(8,128)(2,1)} %stack.2), calls=%async_computation | async-start | bytes 2097152 | tf_op jit(solution)/shard_map/all_to_all | solution.py:54
  25.9 381.3 %all-reduce.2.cloned.1.call-start = ((), (), s32[]{:S(2)}) async-start(), calls=%async_computation.2 | async-start | bytes 1048576 | tf_op jit(solution)/shard_map/psum | solution.py:81
  252.9 190.7 %reduce-scatter.2.cloned.1.call-start = ((), (), s32[]{:S(2)}) async-start(), calls=%async_computation.3 | async-start | bytes 73728 | tf_op jit(solution)/shard_map/reduce_scatter | solution.py:86
  445.1 1.1 copy-start.5
  445.1 1.1 copy-start.6
  445.1 1.1 copy-start.7
Sparse Core Ops, SparseCore 0:
  253.0 154.1 all-reduce.1
  410.6 32.8 reduce-scatter.1
